TPU v7x, 32 devices: a whole 2x2x4 slice. The times are simulated.
32 devices in a mesh: batch: 8 (over z, core), vocab: 4 (over y, x).
Axes of the slice: x: 2, y: 2, z: 4, core: 2. Of those that a mesh axis runs over, the one named last changes fastest.
Arguments:
- hidden: bfloat16 [1024, 4096], P('batch'), may hold values from -40 to 40
- exit_layer: int32 [1024], P('batch'), may hold values from 0 to 7
- exit_gains: float32 [8, 4096], replicated, may hold values from 0.1 to 1.9
- unembed: bfloat16 [4096, 128256], P(None, ('batch', 'vocab')), may hold values from -10 to 10
- targets: int32 [1024], replicated, may hold values from 0 to 128255
- values: float32 [1024], P('batch'), may hold values from -6 to 6
- rewards: float32 [1024], P('batch'), may hold values from -2 to 2
- ref_logprob: float32 [1024], P('batch'), may hold values from -16 to -6
- segment_end: int32 [1024], P('batch'), may hold values 0 or 1
Outputs:
- logprob: float32 [1024], P('batch')
- advantages: float32 [1024], P('batch')
All inputs are finite; a program needn't handle non-finite values. No bound on the sum of `segment_end` on one device may be relied on, other than what follows from the above.
Results may differ from a plain program's by a relative error of at most 0.00054.
Values may be sent and summed in bfloat16 or wider, within the bound.
No kernel may reach another device: no remote copies, remote signals or barrier semaphores. Data moves between devices by JAX's collectives and lax.ppermute only.
A program may use at most 128 MiB of HBM per device.

v0:
```python
import jax
import jax.numpy as jnp
from jax import lax
from jax.sharding import PartitionSpec as P

epsilon_norm = 1e-05
discount = 1.0
trace_decay = 0.999
penalty_weight = 0.1


def joined(part, axis, combine):
    gathered = jax.tree.map(lambda a: lax.all_gather(a, axis), part)

    def take(source):
        return jax.tree.map(lambda a: lax.dynamic_index_in_dim(a, source, 0, False), gathered)

    return lax.fori_loop(
        1, lax.axis_size(axis), lambda source, state: combine(state, take(source)), take(0)
    )


def from_behind(value, axis, steps):
    count = lax.axis_size(axis)
    initial, last = (max(0, -steps), min(count, count - steps))
    return lax.ppermute(value, axis, [(source, source + steps) for source in range(initial, last)])


def normalize(rows, layers, exit_gains):
    states = rows.astype(jnp.float32)
    inverse = lax.rsqrt(jnp.mean(states * states, axis=-1, keepdims=True) + epsilon_norm)
    selector = (
        layers[:, None] == jnp.arange(exit_gains.shape[0], dtype=jnp.int32)[None, :]
    ).astype(jnp.float32)
    scaling = jnp.dot(selector, exit_gains, precision=lax.Precision.HIGHEST)
    return (states * inverse * scaling).astype(jnp.bfloat16)


def per_device(
    hidden, exit_layer, exit_gains, unembed, targets, values, rewards, ref_logprob, segment_end
):
    column_count = unembed.shape[1]
    column_start = lax.axis_index(("batch", "vocab")) * column_count
    columns = jnp.arange(column_count, dtype=jnp.int32)
    total_rows = targets.shape[0]
    owned = hidden.shape[0]
    peers = lax.axis_size("batch")
    width = hidden.shape[1]
    normed = normalize(hidden, exit_layer, exit_gains)
    gathered = lax.all_gather(normed, "batch", axis=0, tiled=True)
    block_rows = 512
    block_count = total_rows // block_rows

    def score_block(pair):
        rows_block, ids_block = pair
        logits = jnp.dot(rows_block, unembed, preferred_element_type=jnp.float32)
        row_max = jnp.max(logits, axis=1)
        row_total = jnp.sum(jnp.exp(logits - row_max[:, None]), axis=1)
        wanted = ids_block - column_start
        picked = jnp.sum(jnp.where(columns[None, :] == wanted[:, None], logits, 0.0), axis=1)
        return (row_max, row_total, picked)

    maxima, totals, picks = lax.map(
        score_block,
        (
            gathered.reshape(block_count, block_rows, width),
            targets.reshape(block_count, block_rows),
        ),
    )
    maxima = maxima.reshape(total_rows)
    totals = totals.reshape(total_rows)
    picks = picks.reshape(total_rows)
    maxima, totals, picks = (
        lax.all_to_all(maxima, "batch", split_axis=0, concat_axis=0, tiled=True),
        lax.all_to_all(totals, "batch", split_axis=0, concat_axis=0, tiled=True),
        lax.all_to_all(picks, "batch", split_axis=0, concat_axis=0, tiled=True),
    )
    maxima = maxima.reshape(peers, owned)
    totals = totals.reshape(peers, owned)
    picks = picks.reshape(peers, owned)
    group_max = jnp.max(maxima, axis=0)
    group_total = jnp.sum(totals * jnp.exp(maxima - group_max[None, :]), axis=0)
    group_pick = jnp.sum(picks, axis=0)

    def combine_groups(first, second):
        larger = jnp.maximum(first[0], second[0])
        summed = first[1] * jnp.exp(first[0] - larger) + second[1] * jnp.exp(second[0] - larger)
        return (larger, summed, first[2] + second[2])

    overall_max, overall_total, overall_pick = joined(
        (group_max, group_total, group_pick), "vocab", combine_groups
    )
    logprob = overall_pick - (overall_max + jnp.log(overall_total))
    following = from_behind(values[:1], "batch", -1)
    next_values = jnp.concatenate([values[1:], following])
    keeping = 1.0 - segment_end.astype(jnp.float32)
    shaped = rewards - penalty_weight * (logprob - ref_logprob)
    deltas = shaped + discount * next_values * keeping - values
    factors = discount * trace_decay * keeping

    def backward(running, inputs):
        factor, delta = inputs
        accrued = delta + factor * running[0]
        product = factor * running[1]
        return ((accrued, product), (accrued, product))

    finished, outputs = lax.scan(
        backward,
        (jnp.zeros((), jnp.float32), jnp.ones((), jnp.float32)),
        (factors, deltas),
        reverse=True,
    )
    local_adv, products = outputs
    head_adv = local_adv[:1]
    head_prod = products[:1]

    def relay_step(index, inbound):
        return from_behind(head_adv + head_prod * inbound, "batch", -1)

    incoming = lax.fori_loop(0, peers - 1, relay_step, jnp.zeros((1,), jnp.float32))
    advantages = local_adv + products * incoming
    return (logprob, advantages)


def solution(mesh):
    placed = (
        P("batch", None),
        P("batch"),
        P(),
        P(None, ("batch", "vocab")),
        P(),
        P("batch"),
        P("batch"),
        P("batch"),
        P("batch"),
    )
    return jax.shard_map(
        per_device, mesh=mesh, in_specs=placed, out_specs=(P("batch"), P("batch")), check_vma=False
    )
```

profile of v0, /device:TPU:1, one launch (start us, length us, event | category | flops | bytes accessed | tf_op | source)
XLA Modules:
  0.0 659.9 jit_solution(1969965212118673331)
XLA Ops:
  8.8 3.4 fusion.13
  12.9 83.9 %all-gather.8.cloned.1.call-done = bf16[1024,4096]{1,0:T(8,128)(2,1)} async-done(((bf16[128,4096]{1,0:T(8,128)(2,1)}), bf16[1024,4096]{1,0:T(8,128)(2,1)}) %all-gather.8.cloned.1.call-update) | async-done | bytes 8388624 | tf_op jit(solution)/shard_map/all_gather | solution.py:50
  96.8 49.9 %while.67 = (s32[]{:T(128)}, f32[2,512]{1,0:T(2,128)S(1)}, f32[2,512]{1,0:T(2,128)S(1)}, f32[2,512]{1,0:T(2,128)S(1)}, bf16[2,512,4096]{2,1,0:T(8,128)(2,1)}, /*...) while((s32[]{:T(128)}, f32[2,512]{1,0:T(2,128)S(1)}, ...), condition=%wide.region_5.6_spmd.clone, body=%wide.region_1.5_spmd.clone.sunk | while | flops 16823081984 | bytes 53471864 | solution.py:63
  96.9 22.6 %fusion.28 = (f32[512]{0:T(512)S(1)}, f32[512,4008]{0,1:T(8,128)S(1)}) fusion(bf16[4096,4008]{0,1:T(8,128)(2,1)} %get-tuple-element.681, bf16[2,512,4096]{2,1,0:T(8,128)(2,1)} %get-tuple-element.680, s32[]{:T(128)} %get-tuple-element.666), kind=kOutput, calls=%fused_computation.38.clone.1 | convolution fusion | flops 16812822528 | bytes 45238784 | tf_op jit(solution)/shard_map/while/body/eval_jaxpr/dot_general | solution.py:56
  119.5 2.2 select_reduce_fusion.2
  121.8 22.6 %fusion.28 = (f32[512]{0:T(512)S(1)}, f32[512,4008]{0,1:T(8,128)S(1)}) fusion(bf16[4096,4008]{0,1:T(8,128)(2,1)} %get-tuple-element.681, bf16[2,512,4096]{2,1,0:T(8,128)(2,1)} %get-tuple-element.680, s32[]{:T(128)} %get-tuple-element.666), kind=kOutput, calls=%fused_computation.38.clone.1 | convolution fusion | flops 16812822528 | bytes 45238784 | tf_op jit(solution)/shard_map/while/body/eval_jaxpr/dot_general | solution.py:56
  144.4 2.2 select_reduce_fusion.2
  147.3 3.4 all-to-all-start
  151.4 4.3 all-to-all-done
  155.7 3.9 all-to-all-start.1
  162.3 2.2 all-to-all-done.1
  164.5 3.9 all-to-all-start.2
  168.4 5.9 all-gather.4
  174.3 5.9 all-gather.5
  180.2 5.0 all-gather.3
  186.4 421.8 %while.65 = (s32[]{:T(128)}, f32[]{:T(128)}, f32[]{:T(128)}, f32[128]{0:T(128)S(1)}, f32[128]{0:T(128)S(1)}, /*index=5*/f32[128]{0:T(128)S(1)}, f32[128]{0:T(128)S(1)}, s32[]{:T(128)}, s32[]{:T(128)}) while((s32[]{:T(128)}, f32[]{:T(128)}, f32[]{:T(128)}, f32[128]{0:T(128)S(1)}, f32[128]{0:T(128)S(1)}, /*index=5*/f32[128]{0:T(128)S(1)}, ...), condition=%wide.region_12.13_spmd, body=%wide.region_11.12_spmd.sunk | while | flops 6 | bytes 189 | solution.py:107
  608.2 44.3 %while.66 = (s32[]{:T(128)}, f32[1]{0:T(128)}, f32[1]{0:T(128)S(1)}, f32[1]{0:T(128)S(1)}, s32[]{:T(128)}) while((s32[]{:T(128)}, f32[1]{0:T(128)}, f32[1]{0:T(128)S(1)}, f32[1]{0:T(128)S(1)}, s32[]{:T(128)}) %tuple.128), condition=%wide.region_14.15_spmd, body=%wide.region_13.14_spmd.sunk | while | flops 4 | bytes 141 | solution.py:120
  608.3 9.0 %collective-permute-start = (f32[1]{0:T(128)}, f32[1]{0:T(128)}, u32[]{:S(2)}, u32[]{:S(2)}) collective-permute-start(f32[1]{0:T(128)} %add.147), channel_id=1, source_target_pairs={{4,0},{8,4},{12,8},{16,12},{20,16},{24,20},{28,24},{5,1},{9,5},{13... | collective-permute-start | bytes 20 | tf_op jit(solution)/shard_map/while/body/eval_jaxpr/ppermute | solution.py:26
  619.8 2.9 collective-permute-start
  625.2 2.9 collective-permute-start
  630.7 2.9 collective-permute-start
  636.2 2.9 collective-permute-start
  641.7 2.9 collective-permute-start
  647.2 2.9 collective-permute-start
  (566 shorter events, 206.5 us)
Async XLA Ops:
  7.2 1.6 copy-start
  7.2 89.7 %all-gather.8.cloned.1.call-start = ((), (), s32[]{:S(2)}) async-start(), calls=%async_computation.3 | async-start | bytes 9437184 | tf_op jit(solution)/shard_map/all_gather | solution.py:50
  96.8 62.7 %copy-start.1 = (f32[128]{0:T(128)S(1)}, f32[128]{0:T(128)}, u32[]{:S(2)}) copy-start(f32[128]{0:T(128)} %param.22) | copy-start | bytes 1540
  96.8 88.4 %copy-start.2 = (f32[128]{0:T(128)S(1)}, f32[128]{0:T(128)}, u32[]{:S(2)}) copy-start(f32[128]{0:T(128)} %param.23) | copy-start | bytes 1540
  96.8 88.4 %copy-start.3 = (f32[128]{0:T(128)S(1)}, f32[128]{0:T(128)}, u32[]{:S(2)}) copy-start(f32[128]{0:T(128)} %param.24) | copy-start | bytes 1540
  96.8 88.4 %copy-start.4 = (s32[128]{0:T(128)S(1)}, s32[128]{0:T(128)}, u32[]{:S(2)}) copy-start(s32[128]{0:T(128)} %param.25) | copy-start | bytes 1540
  147.3 8.4 %all-to-all-start = ((f32[8,128,1]{1,2,0:T(1,128)}), f32[8,128,1]{1,2,0:T(1,128)S(1)}, u32[]{:S(2)}, u32[]{:S(2)}) async-start(f32[8,128,1]{1,2,0:T(1,128)} %all_to_all.18), calls=%async_computation | async-start | bytes 8192 | tf_op jit(solution)/shard_map/all_to_all | solution.py:74
  155.7 8.8 %all-to-all-start.1 = ((f32[8,128,1]{1,2,0:T(1,128)}), f32[8,128,1]{1,2,0:T(1,128)S(1)}, u32[]{:S(2)}, u32[]{:S(2)}) async-start(f32[8,128,1]{1,2,0:T(1,128)} %all_to_all.20), calls=%async_computation.1 | async-start | bytes 8192 | tf_op jit(solution)/shard_map/all_to_all | solution.py:75
  159.6 25.7 %collective-permute-start.1 = (f32[1]{0:T(128)S(1)}, f32[1]{0:T(128)}, u32[]{:S(2)}, u32[]{:S(2)}) collective-permute-start(f32[1]{0:T(128)S(1)} %bitcast.85), channel_id=1, source_target_pairs={{4,0},{8,4},{12,8},{16,12},{20,16},{24,20},{28,24},{5,1},{9,5},{13... | collective-permute-start | bytes 20 | tf_op jit(solution)/shard_map/ppermute | solution.py:26
  164.5 9.8 %all-to-all-start.2 = ((f32[8,128,1]{1,2,0:T(1,128)}), f32[8,128,1]{1,2,0:T(1,128)S(1)}, u32[]{:S(2)}, u32[]{:S(2)}) async-start(f32[8,128,1]{1,2,0:T(1,128)} %all_to_all.22), calls=%async_computation.2 | async-start | bytes 8192 | tf_op jit(solution)/shard_map/all_to_all | solution.py:76
  608.3 10.8 %collective-permute-start = (f32[1]{0:T(128)}, f32[1]{0:T(128)}, u32[]{:S(2)}, u32[]{:S(2)}) collective-permute-start(f32[1]{0:T(128)} %add.147), channel_id=1, source_target_pairs={{4,0},{8,4},{12,8},{16,12},{20,16},{24,20},{28,24},{5,1},{9,5},{13... | collective-permute-start | bytes 20 | tf_op jit(solution)/shard_map/while/body/eval_jaxpr/ppermute | solution.py:26
  619.8 4.8 collective-permute-start
  625.2 4.8 collective-permute-start
  630.7 4.8 collective-permute-start
  636.2 4.8 collective-permute-start
  641.7 4.8 collective-permute-start
  647.2 4.8 collective-permute-start
Sparse Core Ops, SparseCore 0:
  12.3 84.4 all-gather.7
where the time goes:
time: 664 us; the launch traced here: 660 us
  loops' own time  242 us (36%)
  local copies, waits for them, and re-layouts  187 us (28%)
  waiting for transfers between devices  104 us (16%)
  matrix products  48.5 us (7%)
  starting transfers between devices  39.4 us (6%)
  blocking collectives  16.7 us (3%)
  between operations  14.1 us (2%)
  other arithmetic  7.76 us (1%)
    another operation x1, loops' own time, per_device(): lax.scan(backward, (jnp.zeros((), jnp.float32), jnp.ones((), jnp.float32)...  237 us
    dynamic_slice x256, local copies, waits for them, and re-layouts, per_device(): lax.scan(backward, (jnp.zeros((), jnp.float32), jnp.ones((), jnp.float32)...  155 us
    all_gather x1, waiting for transfers between devices, per_device(): gathered = lax.all_gather(normed, 'batch', axis=0, tiled=True)  83.9 us
    dot_general x2, matrix products, score_block(): logits = jnp.dot(rows_block, unembed, preferred_element_type=jnp.float32)  45.2 us
    dynamic_update_slice x256, local copies, waits for them, and re-layouts, per_device(): lax.scan(backward, (jnp.zeros((), jnp.float32), jnp.ones((), jnp.float32)...  29.4 us
    ppermute x8, starting transfers between devices, from_behind(): lax.ppermute(value, axis, [(source, source + steps) for source in range(i...  28.2 us
    all_gather x3, blocking collectives, joined(): gathered = jax.tree.map(lambda a: lax.all_gather(a, axis), part)  16.7 us
    ppermute x8, waiting for transfers between devices, from_behind(): lax.ppermute(value, axis, [(source, source + steps) for source in range(i...  13.7 us
  transfers between devices with their start and end apart: 12, of which 10 were waited for; matrix products, arithmetic and copies ran while one was open for 0% of the time, Pallas kernels for 0%

commit v1 on v0

--- a/solution.py
+++ b/solution.py
@@ -47,7 +47,16 @@
     peers = lax.axis_size("batch")
     width = hidden.shape[1]
     normed = normalize(hidden, exit_layer, exit_gains)
-    gathered = lax.all_gather(normed, "batch", axis=0, tiled=True)
+    value_2 = normed
+    ways, here, turn = (lax.axis_size("batch"), lax.axis_index("batch"), value_2.shape[0])
+    shape = [n * ways if d == 0 else n for d, n in enumerate(value_2.shape)]
+    full = lax.dynamic_update_slice_in_dim(
+        jnp.zeros(shape, value_2.dtype), value_2, here * turn, axis=0
+    )
+    for far in range(1, ways):
+        value_2 = lax.ppermute(value_2, "batch", [(d, (d + 1) % ways) for d in range(ways)])
+        full = lax.dynamic_update_slice_in_dim(full, value_2, (here - far) % ways * turn, axis=0)
+    gathered = full
     block_rows = 512
     block_count = total_rows // block_rows
 

time: 664 us -> 683 us (1.029)
  starting transfers between devices: 39.4 us -> 69.2 us
  between operations: 14.1 us -> 0.81 us
  local copies, waits for them, and re-layouts: 187 us -> 199 us
  waiting for transfers between devices: 104 us -> 95.8 us
    all_gather x1 -> x0, waiting for transfers between devices: 83.9 us -> none  [per_device(): gathered = lax.all_gather(normed, 'batch', axis=0, tiled=True)]
    ppermute x0 -> x7, waiting for transfers between devices: none -> 73.6 us  [per_device(): lax.ppermute(value_2, 'batch', [(d, (d + 1) % ways) for d in range(ways)])]
    ppermute x0 -> x7, starting transfers between devices: none -> 17.5 us  [per_device(): lax.ppermute(value_2, 'batch', [(d, (d + 1) % ways) for d in range(ways)])]
    all_to_all x1, starting transfers between devices: 3.43 us -> 16.6 us  [per_device(): lax.all_to_all(maxima, 'batch', split_axis=0, concat_axis=0, tiled=True)]
    dynamic_update_slice x0 -> x7, local copies, waits for them, and re-layouts: none -> 9.88 us  [per_device(): lax.dynamic_update_slice_in_dim(full, value_2, (here - far) % ways * turn...]
  transfers between devices with their start and end apart: 12 -> 18, of which waited for: 10 -> 16; matrix products, arithmetic and copies ran while one was open for 0% -> 1% of each run, Pallas kernels for 0% -> 0%
where the time goes in v1:
time: 683 us; the launch traced here: 679 us
  loops' own time  242 us (35%)
  local copies, waits for them, and re-layouts  199 us (29%)
  waiting for transfers between devices  95.8 us (14%)
  starting transfers between devices  69.2 us (10%)
  matrix products  47.3 us (7%)
  blocking collectives  17.2 us (3%)
  other arithmetic  7.88 us (1%)
    another operation x1, loops' own time, per_device(): lax.scan(backward, (jnp.zeros((), jnp.float32), jnp.ones((), jnp.float32)...  237 us
    dynamic_slice x256, local copies, waits for them, and re-layouts, per_device(): lax.scan(backward, (jnp.zeros((), jnp.float32), jnp.ones((), jnp.float32)...  153 us
    ppermute x7, waiting for transfers between devices, per_device(): lax.ppermute(value_2, 'batch', [(d, (d + 1) % ways) for d in range(ways)])  73.6 us
    dot_general x2, matrix products, score_block(): logits = jnp.dot(rows_block, unembed, preferred_element_type=jnp.float32)  45.2 us
    dynamic_update_slice x256, local copies, waits for them, and re-layouts, per_device(): lax.scan(backward, (jnp.zeros((), jnp.float32), jnp.ones((), jnp.float32)...  29.4 us
    ppermute x8, starting transfers between devices, from_behind(): lax.ppermute(value, axis, [(source, source + steps) for source in range(i...  27.3 us
    ppermute x7, starting transfers between devices, per_device(): lax.ppermute(value_2, 'batch', [(d, (d + 1) % ways) for d in range(ways)])  17.5 us
    all_gather x3, blocking collectives, joined(): gathered = jax.tree.map(lambda a: lax.all_gather(a, axis), part)  17.2 us
  transfers between devices with their start and end apart: 18, of which 16 were waited for; matrix products, arithmetic and copies ran while one was open for 1% of the time, Pallas kernels for 0%

profile of v1, /device:TPU:1, one launch (start us, length us, event | category | flops | bytes accessed | tf_op | source)
XLA Modules:
  0.0 679.3 jit_solution(4155783967231851121)
XLA Ops:
  2.3 4.3 broadcast_in_dim.43
  11.3 11.7 %collective-permute-done.1 = bf16[128,4096]{1,0:T(8,128)(2,1)S(1)} collective-permute-done((bf16[128,4096]{1,0:T(8,128)(2,1)S(1)}, bf16[128,4096]{1,0:T(8,128)(2,1)S(1)}, u32[]{:S(2)}, u32[]{:S(2)}) %collective-permute-start.1) | collective-permute-done | bytes 1048608 | tf_op jit(solution)/shard_map/ppermute | solution.py:57
  25.6 11.7 %collective-permute-done.2 = bf16[128,4096]{1,0:T(8,128)(2,1)S(1)} collective-permute-done((bf16[128,4096]{1,0:T(8,128)(2,1)S(1)}, bf16[128,4096]{1,0:T(8,128)(2,1)S(1)}, u32[]{:S(2)}, u32[]{:S(2)}) %collective-permute-start.2) | collective-permute-done | bytes 1048608 | tf_op jit(solution)/shard_map/ppermute | solution.py:57
  39.8 11.7 %collective-permute-done.3 = bf16[128,4096]{1,0:T(8,128)(2,1)S(1)} collective-permute-done((bf16[128,4096]{1,0:T(8,128)(2,1)S(1)}, bf16[128,4096]{1,0:T(8,128)(2,1)S(1)}, u32[]{:S(2)}, u32[]{:S(2)}) %collective-permute-start.3) | collective-permute-done | bytes 1048608 | tf_op jit(solution)/shard_map/ppermute | solution.py:57
  54.0 11.7 %collective-permute-done.4 = bf16[128,4096]{1,0:T(8,128)(2,1)S(1)} collective-permute-done((bf16[128,4096]{1,0:T(8,128)(2,1)S(1)}, bf16[128,4096]{1,0:T(8,128)(2,1)S(1)}, u32[]{:S(2)}, u32[]{:S(2)}) %collective-permute-start.4) | collective-permute-done | bytes 1048608 | tf_op jit(solution)/shard_map/ppermute | solution.py:57
  68.3 11.7 %collective-permute-done.5 = bf16[128,4096]{1,0:T(8,128)(2,1)} collective-permute-done((bf16[128,4096]{1,0:T(8,128)(2,1)S(1)}, bf16[128,4096]{1,0:T(8,128)(2,1)}, u32[]{:S(2)}, u32[]{:S(2)}) %collective-permute-start.5) | collective-permute-done | bytes 1048608 | tf_op jit(solution)/shard_map/ppermute | solution.py:57
  87.0 7.6 %collective-permute-done.6 = bf16[128,4096]{1,0:T(8,128)(2,1)S(1)} collective-permute-done((bf16[128,4096]{1,0:T(8,128)(2,1)}, bf16[128,4096]{1,0:T(8,128)(2,1)S(1)}, u32[]{:S(2)}, u32[]{:S(2)}) %collective-permute-start.6) | collective-permute-done | bytes 1048608 | tf_op jit(solution)/shard_map/ppermute | solution.py:57
  101.4 7.3 %collective-permute-done.7 = bf16[128,4096]{1,0:T(8,128)(2,1)S(1)} collective-permute-done((bf16[128,4096]{1,0:T(8,128)(2,1)S(1)}, bf16[128,4096]{1,0:T(8,128)(2,1)S(1)}, u32[]{:S(2)}, u32[]{:S(2)}) %collective-permute-start.7) | collective-permute-done | bytes 1048608 | tf_op jit(solution)/shard_map/ppermute | solution.py:57
  109.8 49.9 %while.67 = (s32[]{:T(128)}, f32[2,512]{1,0:T(2,128)S(1)}, f32[2,512]{1,0:T(2,128)S(1)}, f32[2,512]{1,0:T(2,128)S(1)}, bf16[2,512,4096]{2,1,0:T(8,128)(2,1)}, /*...) while((s32[]{:T(128)}, f32[2,512]{1,0:T(2,128)S(1)}, ...), condition=%wide.region_5.6_spmd.clone, body=%wide.region_1.5_spmd.clone.sunk | while | flops 16823081984 | bytes 53471864 | solution.py:72
  109.8 22.6 %fusion.28 = (f32[512]{0:T(512)S(1)}, f32[512,4008]{0,1:T(8,128)S(1)}) fusion(bf16[4096,4008]{0,1:T(8,128)(2,1)} %get-tuple-element.683, bf16[2,512,4096]{2,1,0:T(8,128)(2,1)} %get-tuple-element.682, s32[]{:T(128)} %get-tuple-element.668), kind=kOutput, calls=%fused_computation.46.clone.1 | convolution fusion | flops 16812822528 | bytes 45238784 | tf_op jit(solution)/shard_map/while/body/eval_jaxpr/dot_general | solution.py:65
  134.8 22.6 %fusion.28 = (f32[512]{0:T(512)S(1)}, f32[512,4008]{0,1:T(8,128)S(1)}) fusion(bf16[4096,4008]{0,1:T(8,128)(2,1)} %get-tuple-element.683, bf16[2,512,4096]{2,1,0:T(8,128)(2,1)} %get-tuple-element.682, s32[]{:T(128)} %get-tuple-element.668), kind=kOutput, calls=%fused_computation.46.clone.1 | convolution fusion | flops 16812822528 | bytes 45238784 | tf_op jit(solution)/shard_map/while/body/eval_jaxpr/dot_general | solution.py:65
  160.3 16.6 %all-to-all-start = ((f32[8,128,1]{1,2,0:T(1,128)}), f32[8,128,1]{1,2,0:T(1,128)S(1)}, u32[]{:S(2)}, u32[]{:S(2)}) async-start(f32[8,128,1]{1,2,0:T(1,128)} %all_to_all.18), calls=%async_computation | async-start | bytes 8192 | tf_op jit(solution)/shard_map/all_to_all | solution.py:83
  177.5 4.3 all-to-all-done
  181.8 3.9 all-to-all-start.1
  190.6 3.9 all-to-all-start.2
  194.5 6.4 all-gather.4
  200.9 5.9 all-gather.5
  206.8 4.9 all-gather.3
  213.1 419.8 %while.65 = (s32[]{:T(128)}, f32[]{:T(128)}, f32[]{:T(128)}, f32[128]{0:T(128)S(1)}, f32[128]{0:T(128)S(1)}, /*index=5*/f32[128]{0:T(128)S(1)}, f32[128]{0:T(128)S(1)}, s32[]{:T(128)}, s32[]{:T(128)}) while((s32[]{:T(128)}, f32[]{:T(128)}, f32[]{:T(128)}, f32[128]{0:T(128)S(1)}, f32[128]{0:T(128)S(1)}, /*index=5*/f32[128]{0:T(128)S(1)}, ...), condition=%wide.region_12.13_spmd, body=%wide.region_11.12_spmd.sunk | while | flops 6 | bytes 189 | solution.py:116
  632.9 45.9 %while.66 = (s32[]{:T(128)}, f32[1]{0:T(128)}, f32[1]{0:T(128)S(1)}, f32[1]{0:T(128)S(1)}, s32[]{:T(128)}) while((s32[]{:T(128)}, f32[1]{0:T(128)}, f32[1]{0:T(128)S(1)}, f32[1]{0:T(128)S(1)}, s32[]{:T(128)}) %tuple.127), condition=%wide.region_14.15_spmd, body=%wide.region_13.14_spmd.sunk | while | flops 4 | bytes 141 | solution.py:129
  633.0 8.9 %collective-permute-start = (f32[1]{0:T(128)}, f32[1]{0:T(128)}, u32[]{:S(2)}, u32[]{:S(2)}) collective-permute-start(f32[1]{0:T(128)} %add.215), channel_id=1, source_target_pairs={{4,0},{8,4},{12,8},{16,12},{20,16},{24,20},{28,24},{5,1},{9,5},{13... | collective-permute-start | bytes 20 | tf_op jit(solution)/shard_map/while/body/eval_jaxpr/ppermute | solution.py:26
  644.7 2.7 collective-permute-start
  656.1 2.7 collective-permute-start
  661.8 2.7 collective-permute-start
  (593 shorter events, 250.4 us)
Async XLA Ops:
  0.7 67.6 %copy-start.3 = (s32[1024]{0:T(1024)S(1)}, s32[1024]{0:T(1024)}, u32[]{:S(2)}) copy-start(s32[1024]{0:T(1024)} %param.21) | copy-start | bytes 12292
  8.7 14.4 %collective-permute-start.1 = (bf16[128,4096]{1,0:T(8,128)(2,1)S(1)}, bf16[128,4096]{1,0:T(8,128)(2,1)S(1)}, u32[]{:S(2)}, u32[]{:S(2)}) collective-permute-start(bf16[128,4096]{1,0:T(8,128)(2,1)S(1)} %get-tuple-element.483), channel_id=1, source_target_pairs={{0,4},{4,8},{8,12},{12,16},{16,20},{20,24},{24,28},{28,0},{1,5},{5... | collective-permute-start | bytes 3145736 | tf_op jit(solution)/shard_map/ppermute | solution.py:57
  23.1 14.2 %collective-permute-start.2 = (bf16[128,4096]{1,0:T(8,128)(2,1)S(1)}, bf16[128,4096]{1,0:T(8,128)(2,1)S(1)}, u32[]{:S(2)}, u32[]{:S(2)}) collective-permute-start(bf16[128,4096]{1,0:T(8,128)(2,1)S(1)} %collective-permute-done.1), channel_id=1, source_target_pairs={{0,4},{4,8},{8,12},{12,16},{16,20},{20,24},{24,28},{28,0},{1,5},{5... | collective-permute-start | bytes 3145736 | tf_op jit(solution)/shard_map/ppermute | solution.py:57
  37.3 14.2 %collective-permute-start.3 = (bf16[128,4096]{1,0:T(8,128)(2,1)S(1)}, bf16[128,4096]{1,0:T(8,128)(2,1)S(1)}, u32[]{:S(2)}, u32[]{:S(2)}) collective-permute-start(bf16[128,4096]{1,0:T(8,128)(2,1)S(1)} %collective-permute-done.2), channel_id=1, source_target_pairs={{0,4},{4,8},{8,12},{12,16},{16,20},{20,24},{24,28},{28,0},{1,5},{5... | collective-permute-start | bytes 3145736 | tf_op jit(solution)/shard_map/ppermute | solution.py:57
  51.5 14.2 %copy-start.2 = (bf16[128,4096]{1,0:T(8,128)(2,1)}, bf16[128,4096]{1,0:T(8,128)(2,1)S(1)}, u32[]{:S(2)}) copy-start(bf16[128,4096]{1,0:T(8,128)(2,1)S(1)} %collective-permute-done.3) | copy-start | bytes 3145732
  51.5 14.2 %collective-permute-start.4 = (bf16[128,4096]{1,0:T(8,128)(2,1)S(1)}, bf16[128,4096]{1,0:T(8,128)(2,1)S(1)}, u32[]{:S(2)}, u32[]{:S(2)}) collective-permute-start(bf16[128,4096]{1,0:T(8,128)(2,1)S(1)} %collective-permute-done.3), channel_id=1, source_target_pairs={{0,4},{4,8},{8,12},{12,16},{16,20},{20,24},{24,28},{28,0},{1,5},{5... | collective-permute-start | bytes 3145736 | tf_op jit(solution)/shard_map/ppermute | solution.py:57
  65.8 14.2 %collective-permute-start.5 = (bf16[128,4096]{1,0:T(8,128)(2,1)S(1)}, bf16[128,4096]{1,0:T(8,128)(2,1)}, u32[]{:S(2)}, u32[]{:S(2)}) collective-permute-start(bf16[128,4096]{1,0:T(8,128)(2,1)S(1)} %collective-permute-done.4), channel_id=1, source_target_pairs={{0,4},{4,8},{8,12},{12,16},{16,20},{20,24},{24,28},{28,0},{1,5},{5... | collective-permute-start | bytes 3145736 | tf_op jit(solution)/shard_map/ppermute | solution.py:57
  80.0 14.6 %collective-permute-start.6 = (bf16[128,4096]{1,0:T(8,128)(2,1)}, bf16[128,4096]{1,0:T(8,128)(2,1)S(1)}, u32[]{:S(2)}, u32[]{:S(2)}) collective-permute-start(bf16[128,4096]{1,0:T(8,128)(2,1)} %collective-permute-done.5), channel_id=1, source_target_pairs={{0,4},{4,8},{8,12},{12,16},{16,20},{20,24},{24,28},{28,0},{1,5},{5... | collective-permute-start | bytes 3145736 | tf_op jit(solution)/shard_map/ppermute | solution.py:57
  94.6 14.1 %collective-permute-start.7 = (bf16[128,4096]{1,0:T(8,128)(2,1)S(1)}, bf16[128,4096]{1,0:T(8,128)(2,1)S(1)}, u32[]{:S(2)}, u32[]{:S(2)}) collective-permute-start(bf16[128,4096]{1,0:T(8,128)(2,1)S(1)} %collective-permute-done.6), channel_id=1, source_target_pairs={{0,4},{4,8},{8,12},{12,16},{16,20},{20,24},{24,28},{28,0},{1,5},{5... | collective-permute-start | bytes 3145736 | tf_op jit(solution)/shard_map/ppermute | solution.py:57
  109.8 75.9 %copy-start.5 = (f32[128]{0:T(128)S(1)}, f32[128]{0:T(128)}, u32[]{:S(2)}) copy-start(f32[128]{0:T(128)} %param.22) | copy-start | bytes 1540
  109.8 102.1 %copy-start.6 = (f32[128]{0:T(128)S(1)}, f32[128]{0:T(128)}, u32[]{:S(2)}) copy-start(f32[128]{0:T(128)} %param.23) | copy-start | bytes 1540
  109.8 102.1 %copy-start.7 = (f32[128]{0:T(128)S(1)}, f32[128]{0:T(128)}, u32[]{:S(2)}) copy-start(f32[128]{0:T(128)} %param.24) | copy-start | bytes 1540
  109.8 102.1 %copy-start.8 = (s32[128]{0:T(128)S(1)}, s32[128]{0:T(128)}, u32[]{:S(2)}) copy-start(s32[128]{0:T(128)} %param.25) | copy-start | bytes 1540
  160.3 21.5 %all-to-all-start = ((f32[8,128,1]{1,2,0:T(1,128)}), f32[8,128,1]{1,2,0:T(1,128)S(1)}, u32[]{:S(2)}, u32[]{:S(2)}) async-start(f32[8,128,1]{1,2,0:T(1,128)} %all_to_all.18), calls=%async_computation | async-start | bytes 8192 | tf_op jit(solution)/shard_map/all_to_all | solution.py:83
  181.8 8.8 %all-to-all-start.1 = ((f32[8,128,1]{1,2,0:T(1,128)}), f32[8,128,1]{1,2,0:T(1,128)S(1)}, u32[]{:S(2)}, u32[]{:S(2)}) async-start(f32[8,128,1]{1,2,0:T(1,128)} %all_to_all.20), calls=%async_computation.1 | async-start | bytes 8192 | tf_op jit(solution)/shard_map/all_to_all | solution.py:84
  185.7 26.2 %collective-permute-start.8 = (f32[1]{0:T(128)S(1)}, f32[1]{0:T(128)}, u32[]{:S(2)}, u32[]{:S(2)}) collective-permute-start(f32[1]{0:T(128)S(1)} %bitcast.85), channel_id=1, source_target_pairs={{4,0},{8,4},{12,8},{16,12},{20,16},{24,20},{28,24},{5,1},{9,5},{13... | collective-permute-start | bytes 20 | tf_op jit(solution)/shard_map/ppermute | solution.py:26
  190.6 10.3 %all-to-all-start.2 = ((f32[8,128,1]{1,2,0:T(1,128)}), f32[8,128,1]{1,2,0:T(1,128)S(1)}, u32[]{:S(2)}, u32[]{:S(2)}) async-start(f32[8,128,1]{1,2,0:T(1,128)} %all_to_all.22), calls=%async_computation.2 | async-start | bytes 8192 | tf_op jit(solution)/shard_map/all_to_all | solution.py:85
  633.0 11.0 %collective-permute-start = (f32[1]{0:T(128)}, f32[1]{0:T(128)}, u32[]{:S(2)}, u32[]{:S(2)}) collective-permute-start(f32[1]{0:T(128)} %add.215), channel_id=1, source_target_pairs={{4,0},{8,4},{12,8},{16,12},{20,16},{24,20},{28,24},{5,1},{9,5},{13... | collective-permute-start | bytes 20 | tf_op jit(solution)/shard_map/while/body/eval_jaxpr/ppermute | solution.py:26
  644.7 5.0 collective-permute-start
  650.4 5.0 collective-permute-start
  656.1 5.0 collective-permute-start
  661.8 5.0 collective-permute-start
  667.5 5.0 collective-permute-start
  673.2 5.0 collective-permute-start
  (3 other events, 17.8 us)
